TPU v7x, 32 devices: a whole 2x2x4 slice. The times are simulated.
32 devices in a mesh: seq: 8 (over z, x), head: 4 (over y, core).
Axes of the slice: x: 2, y: 2, z: 4, core: 2. Of those that a mesh axis runs over, the one named last changes fastest.
Arguments:
- block_input: bfloat16 [4096, 2048], P(('seq', 'head')), may hold values from -6 to 6
- norm1_gain: float32 [2048], replicated, may hold values from 0.5 to 1.5
- query_weight: bfloat16 [2048, 2048], P(None, 'head'), may hold values from -0.125 to 0.125
- key_weight: bfloat16 [2048, 2048], P(None, 'head'), may hold values from -0.125 to 0.125
- value_weight: bfloat16 [2048, 2048], P(None, 'head'), may hold values from -0.125 to 0.125
- gate_weight: bfloat16 [2048, 2048], P(None, 'head'), may hold values from -0.125 to 0.125
- rate_weight: bfloat16 [2048, 32], P(None, 'head'), may hold values from -0.125 to 0.125
- rate_bias: float32 [32], P('head'), may hold values from -3 to 3
- rate_scale: float32 [32], P('head'), may hold values from 7.324219e-05 to 0.008
- init_state: float32 [32, 64, 64], P('head'), may hold values from -0.75 to 0.75
- init_bias: float32 [32, 64], P('head'), may hold values from -5 to 5
- post_gain: float32 [2048], P('head'), may hold values from 0.5 to 1.5
- post_bias: float32 [2048], P('head'), may hold values from -3 to 3
- out_weight: bfloat16 [2048, 2048], P('head'), may hold values from -0.25 to 0.25
- norm2_gain: float32 [2048], replicated, may hold values from 0.5 to 1.5
- mlp_gate: bfloat16 [2048, 5504], P(None, 'head'), may hold values from -0.125 to 0.125
- mlp_up: bfloat16 [2048, 5504], P(None, 'head'), may hold values from -0.125 to 0.125
- mlp_down: bfloat16 [5504, 2048], P('head'), may hold values from -0.15625 to 0.15625
- out_cotangent: bfloat16 [4096, 2048], P(('seq', 'head')), may hold values from -6 to 6
Outputs:
- block_out: bfloat16 [4096, 2048], P(('seq', 'head'))
- input_grad: float32 [4096, 2048], P(('seq', 'head'))
- norm1_gain_grad: float32 [2048], replicated
- query_weight_grad: float32 [2048, 2048], P(None, 'head')
- key_weight_grad: float32 [2048, 2048], P(None, 'head')
- value_weight_grad: float32 [2048, 2048], P(None, 'head')
- gate_weight_grad: float32 [2048, 2048], P(None, 'head')
- rate_weight_grad: float32 [2048, 32], P(None, 'head')
- rate_bias_grad: float32 [32], P('head')
- rate_scale_grad: float32 [32], P('head')
- init_state_grad: float32 [32, 64, 64], P('head')
- init_bias_grad: float32 [32, 64], P('head')
- post_gain_grad: float32 [2048], P('head')
- post_bias_grad: float32 [2048], P('head')
- out_weight_grad: float32 [2048, 2048], P('head')
- norm2_gain_grad: float32 [2048], replicated
- mlp_gate_grad: float32 [2048, 5504], P(None, 'head')
- mlp_up_grad: float32 [2048, 5504], P(None, 'head')
- mlp_down_grad: float32 [5504, 2048], P('head')
All inputs are finite; a program needn't handle non-finite values.
Results may differ from a plain program's by a relative error of at most 0.025.
Values may be sent and summed in bfloat16 or wider, within the bound.
No kernel may reach another device: no remote copies, remote signals or barrier semaphores. Data moves between devices by JAX's collectives and lax.ppermute only.
A program may use at most 256 MiB of HBM per device.

v0:
```python
import jax
import jax.numpy as jnp
from jax import lax
from jax.sharding import PartitionSpec as P

MB = 16
HIGHEST = lax.Precision.HIGHEST
EPSILON = 1e-06


def passed_along(shard, axis, by):
    size = lax.axis_size(axis)
    pairs = [(i, i + by) for i in range(size) if 0 <= i + by < size]
    return lax.ppermute(shard, axis, pairs)


def augment(values):
    ones_col = jnp.ones(values.shape[:-1] + (1,), jnp.float32)
    return jnp.concatenate([values, ones_col], axis=-1)


def compose(earlier, later):
    matrix = jnp.einsum("...ij,...jk->...ik", later[0], earlier[0], precision=HIGHEST)
    offset = jnp.einsum("...ij,...jk->...ik", later[0], earlier[1], precision=HIGHEST) + later[1]
    return (matrix, offset)


def apply_map(matrix, offset, inner_state):
    return jnp.einsum("...ij,...jk->...ik", matrix, inner_state, precision=HIGHEST) + offset


def step_matrix_of(key_block, rate_block):
    key_aug = augment(key_block)
    weighted_keys = key_aug * rate_block[..., None]
    identity = jnp.eye(key_aug.shape[-1], dtype=jnp.float32)
    return (
        identity - jnp.einsum("hni,hnj->hij", weighted_keys, key_aug, precision=HIGHEST),
        weighted_keys,
    )


def segment_map(identity, zero_state, key_blocks, value_blocks, rate_blocks):

    def turn(carry, inputs):
        key_block, value_block, rate_block = inputs
        step_matrix, weighted_keys = step_matrix_of(key_block, rate_block)
        step_offset = jnp.einsum(
            "hni,hno->hio", weighted_keys, value_block - key_block, precision=HIGHEST
        )
        return (compose(carry, (step_matrix, step_offset)), None)

    result, unused = lax.scan(turn, (identity, zero_state), (key_blocks, value_blocks, rate_blocks))
    return result


def causal_weights(query_block, key_block, rate_block):
    query_aug = augment(query_block)
    key_aug = augment(key_block)
    scores = jnp.einsum("hmi,hni->hmn", query_aug, key_aug, precision=HIGHEST)
    causal_mask = jnp.tril(jnp.ones((scores.shape[1], scores.shape[2]), jnp.float32))
    return (query_aug, key_aug, scores * causal_mask * rate_block[:, None, :])


def inner_block(inner_state, inputs):
    query_block, key_block, value_block, rate_block = inputs
    query_aug, key_aug, weighted = causal_weights(query_block, key_block, rate_block)
    errors = jnp.einsum("hmi,hio->hmo", key_aug, inner_state, precision=HIGHEST) - (
        value_block - key_block
    )
    outputs = (
        query_block
        + jnp.einsum("hmi,hio->hmo", query_aug, inner_state, precision=HIGHEST)
        - jnp.einsum("hmn,hno->hmo", weighted, errors, precision=HIGHEST)
    )
    new_state = inner_state - jnp.einsum(
        "hni,hno->hio", key_aug * rate_block[:, :, None], errors, precision=HIGHEST
    )
    return (new_state, outputs)


def segment_run(state_in, query_blocks, key_blocks, value_blocks, rate_blocks):
    last_state, outputs = lax.scan(
        jax.checkpoint(inner_block), state_in, (query_blocks, key_blocks, value_blocks, rate_blocks)
    )
    return (outputs, last_state)


def local_state_grad(zero_state, query_blocks, key_blocks, rate_blocks, d_z_blocks):

    def turn(pending, inputs):
        query_block, key_block, rate_block, d_z_block = inputs
        query_aug, key_aug, weighted = causal_weights(query_block, key_block, rate_block)
        back_errors = jnp.einsum("hmn,hmo->hno", weighted, d_z_block, precision=HIGHEST)
        direct = jnp.einsum("hmi,hmo->hio", query_aug, d_z_block, precision=HIGHEST) - jnp.einsum(
            "hni,hno->hio", key_aug, back_errors, precision=HIGHEST
        )
        step_matrix, unused = step_matrix_of(key_block, rate_block)
        return (jnp.einsum("hji,hjo->hio", step_matrix, pending, precision=HIGHEST) + direct, None)

    result, unused = lax.scan(
        turn, zero_state, (query_blocks, key_blocks, rate_blocks, d_z_blocks), reverse=True
    )
    return result


def to_heads(values, local_heads, head_width):
    return values.reshape(-1, MB, local_heads, head_width).transpose(0, 2, 1, 3)


def from_heads(values):
    block_count, head_count, block_size, head_width = values.shape
    return values.transpose(0, 2, 1, 3).reshape(block_count * block_size, head_count * head_width)


def gelu_tanh(values):
    return jax.nn.gelu(values, approximate=True)


def relay_state(values, offset):
    return passed_along(values, "seq", offset)


def body(
    block_input,
    norm1_gain,
    query_weight,
    key_weight,
    value_weight,
    gate_weight,
    rate_weight,
    rate_bias,
    rate_scale,
    init_state,
    init_bias,
    post_gain,
    post_bias,
    out_weight,
    norm2_gain,
    mlp_gate,
    mlp_up,
    mlp_down,
    out_cotangent,
):
    local_heads = init_state.shape[0]
    head_width = init_state.shape[1]
    model_width = block_input.shape[1]
    seq_index = lax.axis_index("seq")
    seq_count = lax.axis_size("seq")
    input_f32 = block_input.astype(jnp.float32)
    scale_in = lax.rsqrt(jnp.mean(input_f32 * input_f32, axis=-1, keepdims=True) + EPSILON)
    unit_in = input_f32 * scale_in
    normed = (unit_in * norm1_gain).astype(jnp.bfloat16)
    group_in, group_cot = (
        lax.all_gather(normed, "head", axis=0, tiled=True),
        lax.all_gather(out_cotangent, "head", axis=0, tiled=True),
    )
    query_rows = jnp.dot(group_in, query_weight, preferred_element_type=jnp.float32)
    key_rows = jnp.dot(group_in, key_weight, preferred_element_type=jnp.float32)
    value_rows = jnp.dot(group_in, value_weight, preferred_element_type=jnp.float32)
    gate_pre = jnp.dot(group_in, gate_weight, preferred_element_type=jnp.float32)
    rate_pre = jnp.dot(group_in, rate_weight, preferred_element_type=jnp.float32) + rate_bias
    rate_sig = jax.nn.sigmoid(rate_pre)
    rate_rows = rate_sig * rate_scale
    query_blocks = to_heads(query_rows, local_heads, head_width)
    key_blocks = to_heads(key_rows, local_heads, head_width)
    value_blocks = to_heads(value_rows, local_heads, head_width)
    rate_blocks = rate_rows.reshape(-1, MB, local_heads).transpose(0, 2, 1)
    aug_width = head_width + 1
    identity = jnp.broadcast_to(
        jnp.eye(aug_width, dtype=jnp.float32), (local_heads, aug_width, aug_width)
    )
    start_state = jnp.concatenate([init_state, init_bias[:, None, :]], axis=1)
    zero_state = jnp.zeros_like(start_state)
    segment_matrix, segment_offset = segment_map(
        identity, zero_state, key_blocks, value_blocks, rate_blocks
    )

    def forward_turn(turn, incoming):
        received = relay_state(apply_map(segment_matrix, segment_offset, incoming), 1)
        return jnp.where(seq_index == 0, start_state, received)

    state_in = lax.fori_loop(0, seq_count - 1, forward_turn, start_state)
    (z_blocks, last_state), inner_pullback = jax.vjp(
        segment_run, state_in, query_blocks, key_blocks, value_blocks, rate_blocks
    )
    z_rows = from_heads(z_blocks)
    stat_sums = lax.psum((jnp.sum(z_rows, axis=-1), jnp.sum(z_rows * z_rows, axis=-1)), "head")
    row_mean = stat_sums[0] / model_width
    row_var = stat_sums[1] / model_width - row_mean * row_mean
    inv_scale = lax.rsqrt(row_var + EPSILON)[:, None]
    z_hat = (z_rows - row_mean[:, None]) * inv_scale
    post_out = z_hat * post_gain + post_bias
    gate_act, gelu_back = jax.vjp(gelu_tanh, gate_pre)
    gated_out = (gate_act * post_out).astype(jnp.bfloat16)
    picked = gated_out
    attn_out = lax.psum_scatter(
        jnp.dot(picked, out_weight, preferred_element_type=jnp.float32).astype(jnp.bfloat16),
        "head",
        scatter_dimension=0,
        tiled=True,
    ).astype(jnp.float32)
    middle = input_f32 + attn_out
    scale_mid = lax.rsqrt(jnp.mean(middle * middle, axis=-1, keepdims=True) + EPSILON)
    unit_mid = middle * scale_mid
    mlp_input = (unit_mid * norm2_gain).astype(jnp.bfloat16)
    mlp_group = lax.all_gather(mlp_input, "head", axis=0, tiled=True)
    gate_mlp = jnp.dot(mlp_group, mlp_gate, preferred_element_type=jnp.float32)
    up_mlp = jnp.dot(mlp_group, mlp_up, preferred_element_type=jnp.float32)
    silu_gate, silu_back = jax.vjp(jax.nn.silu, gate_mlp)
    hidden = (silu_gate * up_mlp).astype(jnp.bfloat16)
    picked = hidden
    mlp_out = lax.psum_scatter(
        jnp.dot(picked, mlp_down, preferred_element_type=jnp.float32).astype(jnp.bfloat16),
        "head",
        scatter_dimension=0,
        tiled=True,
    ).astype(jnp.float32)
    block_out = (middle + mlp_out).astype(jnp.bfloat16)
    cot_f32 = out_cotangent.astype(jnp.float32)
    d_hidden = jnp.dot(group_cot, mlp_down.T, preferred_element_type=jnp.float32)
    mlp_down_grad = jnp.dot(hidden.T, group_cot, preferred_element_type=jnp.float32)
    d_gate_mlp = silu_back(d_hidden * up_mlp)[0].astype(jnp.bfloat16)
    d_up_mlp = (d_hidden * silu_gate).astype(jnp.bfloat16)
    mlp_gate_grad = jnp.dot(mlp_group.T, d_gate_mlp, preferred_element_type=jnp.float32)
    mlp_up_grad = jnp.dot(mlp_group.T, d_up_mlp, preferred_element_type=jnp.float32)
    d_mlp_input = lax.psum_scatter(
        jnp.dot(d_gate_mlp, mlp_gate.T, preferred_element_type=jnp.float32)
        + jnp.dot(d_up_mlp, mlp_up.T, preferred_element_type=jnp.float32),
        "head",
        scatter_dimension=0,
        tiled=True,
    )
    scaled_mid = d_mlp_input * norm2_gain
    norm2_part = jnp.sum(d_mlp_input * unit_mid, axis=0)
    d_middle = cot_f32 + scale_mid * (
        scaled_mid - unit_mid * jnp.mean(scaled_mid * unit_mid, axis=-1, keepdims=True)
    )
    d_attn = d_middle.astype(jnp.bfloat16)
    d_attn_group = lax.all_gather(d_attn, "head", axis=0, tiled=True)
    d_gated = jnp.dot(d_attn_group, out_weight.T, preferred_element_type=jnp.float32)
    out_weight_grad = jnp.dot(gated_out.T, d_attn_group, preferred_element_type=jnp.float32)
    d_post = d_gated * gate_act
    d_gate_pre = gelu_back(d_gated * post_out)[0].astype(jnp.bfloat16)
    post_gain_part = jnp.sum(d_post * z_hat, axis=0)
    post_bias_part = jnp.sum(d_post, axis=0)
    d_zhat = d_post * post_gain
    back_sums = lax.psum((jnp.sum(d_zhat, axis=-1), jnp.sum(d_zhat * z_hat, axis=-1)), "head")
    d_z = inv_scale * (
        d_zhat - back_sums[0][:, None] / model_width - z_hat * (back_sums[1][:, None] / model_width)
    )
    d_z_blocks = to_heads(d_z, local_heads, head_width)
    local_state = local_state_grad(zero_state, query_blocks, key_blocks, rate_blocks, d_z_blocks)
    back_matrix = jnp.swapaxes(segment_matrix, 1, 2)

    def backward_turn(turn, pending):
        return relay_state(apply_map(back_matrix, local_state, pending), -1)

    grad_out = lax.fori_loop(0, seq_count - 1, backward_turn, zero_state)
    all_terms = inner_pullback((d_z_blocks, grad_out))
    init_part = jnp.where(seq_index == 0, all_terms[0], 0.0)
    d_query = from_heads(all_terms[1]).astype(jnp.bfloat16)
    d_key = from_heads(all_terms[2]).astype(jnp.bfloat16)
    d_value = from_heads(all_terms[3]).astype(jnp.bfloat16)
    d_rate = all_terms[4].transpose(0, 2, 1).reshape(-1, local_heads)
    d_rate_pre = (d_rate * rate_scale * rate_sig * (1.0 - rate_sig)).astype(jnp.bfloat16)
    scale_part = jnp.sum(d_rate * rate_sig, axis=0)
    rate_bias_part = jnp.sum(d_rate_pre.astype(jnp.float32), axis=0)
    query_grad = jnp.dot(group_in.T, d_query, preferred_element_type=jnp.float32)
    key_grad = jnp.dot(group_in.T, d_key, preferred_element_type=jnp.float32)
    value_grad = jnp.dot(group_in.T, d_value, preferred_element_type=jnp.float32)
    gate_grad = jnp.dot(group_in.T, d_gate_pre, preferred_element_type=jnp.float32)
    rate_weight_part = jnp.dot(group_in.T, d_rate_pre, preferred_element_type=jnp.float32)

    def picked(values):
        return values

    total = jnp.dot(picked(d_query), query_weight.T, preferred_element_type=jnp.float32)
    total = total + jnp.dot(picked(d_key), key_weight.T, preferred_element_type=jnp.float32)
    total = total + jnp.dot(picked(d_value), value_weight.T, preferred_element_type=jnp.float32)
    total = total + jnp.dot(picked(d_gate_pre), gate_weight.T, preferred_element_type=jnp.float32)
    d_normed = lax.psum_scatter(
        (
            total + jnp.dot(picked(d_rate_pre), rate_weight.T, preferred_element_type=jnp.float32)
        ).astype(jnp.bfloat16),
        "head",
        scatter_dimension=0,
        tiled=True,
    ).astype(jnp.float32)
    scaled_in = d_normed * norm1_gain
    norm1_part = jnp.sum(d_normed * unit_in, axis=0)
    input_grad = d_middle + scale_in * (
        scaled_in - unit_in * jnp.mean(scaled_in * unit_in, axis=-1, keepdims=True)
    )
    summed = (
        lax.psum(query_grad.astype(jnp.bfloat16), "seq").astype(jnp.float32),
        lax.psum(key_grad.astype(jnp.bfloat16), "seq").astype(jnp.float32),
        lax.psum(value_grad.astype(jnp.bfloat16), "seq").astype(jnp.float32),
        lax.psum(gate_grad.astype(jnp.bfloat16), "seq").astype(jnp.float32),
        lax.psum(rate_weight_part.astype(jnp.bfloat16), "seq").astype(jnp.float32),
        lax.psum(rate_bias_part.astype(jnp.bfloat16), "seq").astype(jnp.float32),
        lax.psum(scale_part.astype(jnp.bfloat16), "seq").astype(jnp.float32),
        lax.psum(init_part.astype(jnp.bfloat16), "seq").astype(jnp.float32),
        lax.psum(post_gain_part.astype(jnp.bfloat16), "seq").astype(jnp.float32),
        lax.psum(post_bias_part.astype(jnp.bfloat16), "seq").astype(jnp.float32),
        lax.psum(out_weight_grad.astype(jnp.bfloat16), "seq").astype(jnp.float32),
        lax.psum(mlp_gate_grad.astype(jnp.bfloat16), "seq").astype(jnp.float32),
        lax.psum(mlp_up_grad.astype(jnp.bfloat16), "seq").astype(jnp.float32),
        lax.psum(mlp_down_grad.astype(jnp.bfloat16), "seq").astype(jnp.float32),
    )
    gain_grads = lax.psum((norm1_part, norm2_part), ("seq", "head"))
    init_total = summed[7]
    return (
        block_out,
        input_grad,
        gain_grads[0],
        summed[0],
        summed[1],
        summed[2],
        summed[3],
        summed[4],
        summed[5],
        summed[6],
        init_total[:, :head_width, :],
        init_total[:, head_width, :],
        summed[8],
        summed[9],
        summed[10],
        gain_grads[1],
        summed[11],
        summed[12],
        summed[13],
    )


def solution(mesh):
    in_specs = (
        P(("seq", "head"), None),
        P(),
        P(None, "head"),
        P(None, "head"),
        P(None, "head"),
        P(None, "head"),
        P(None, "head"),
        P("head"),
        P("head"),
        P("head", None, None),
        P("head", None),
        P("head"),
        P("head"),
        P("head", None),
        P(),
        P(None, "head"),
        P(None, "head"),
        P("head", None),
        P(("seq", "head"), None),
    )
    out_specs = (
        P(("seq", "head"), None),
        P(("seq", "head"), None),
        P(),
        P(None, "head"),
        P(None, "head"),
        P(None, "head"),
        P(None, "head"),
        P(None, "head"),
        P("head"),
        P("head"),
        P("head", None, None),
        P("head", None),
        P("head"),
        P("head"),
        P("head", None),
        P(),
        P(None, "head"),
        P(None, "head"),
        P("head", None),
    )
    return jax.shard_map(body, mesh=mesh, in_specs=in_specs, out_specs=out_specs, check_vma=False)
```

profile of v0, /device:TPU:0, one launch (start us, length us, event | category | flops | bytes accessed | tf_op | source)
XLA Modules:
  0.0 2290.9 jit_solution(17241817064741074859)
XLA Ops:
  11.3 24.8 %all-gather.5.cloned.1.call-done = bf16[512,2048]{1,0:T(8,128)(2,1)} async-done(((bf16[128,2048]{1,0:T(8,128)(2,1)}), bf16[512,2048]{1,0:T(8,128)(2,1)}) %all-gather.5.cloned.1.call-update) | async-done | bytes 2097168 | tf_op jit(solution)/shard_map/all_gather | solution.py:154
  39.3 4.4 fusion.137
  62.0 5.2 copy_bitcast_fusion.2
  67.1 164.2 %while.97 = (s32[]{:T(128)}, f32[8,65,65]{2,1,0:T(8,128)S(1)}, f32[8,65,64]{1,2,0:T(8,128)S(1)}, f32[32,8,16,64]{3,2,1,0:T(8,128)}, f32[32,8,16]{2,1,0:T(8,128)}, /*index=5*/f32[32,8,16,64]{3,2,1,0:T(8,128)}) while((s32[]{:T(128)}, f32[8,65,65]{2,1,0:T(8,128)S(1)}, f32[8,65,64]{1,2,0:T(8,128)S(1)}, ...), condition=%wide.region_2.3_spmd.clone.clone, body=%wide.region_1.2_spmd.clone.sunk.clone | while | flops 65335404 | bytes 1942347 | solution.py:52
  231.3 75.0 %while.93 = (s32[]{:T(128)}, f32[8,65,64]{1,2,0:T(8,128)S(1)}, pred[]{:T(512)}, f32[8,65,65]{2,1,0:T(8,128)S(1)}, f32[8,65,64]{1,2,0:T(8,128)S(1)}, /*index=5*/f32[8,65,64]{1,2,0:T(8,128)S(1)}) while((s32[]{:T(128)}, f32[8,65,64]{1,2,0:T(8,128)S(1)}, pred[]{:T(512)}, f32[8,65,65]{2,1,0:T(8,128)S(1)}, f32[8,65,64]{1,2,0:T(8,128)S(1)}, ...), condition=%wide.region_4.5_spmd.clone, body=%wide.region_3.4_spmd.sunk.clone | while | flops 26024960 | bytes 1466510 | solution.py:182
  236.0 6.3 collective-permute-done
  247.9 5.4 collective-permute-done
  259.0 4.5 collective-permute-done
  264.9 5.2 collective-permute-start
  275.6 5.2 collective-permute-start
  286.3 5.2 collective-permute-start
  297.0 5.2 collective-permute-start
  306.4 189.6 %while.96 = (s32[]{:T(128)}, f32[8,65,64]{1,2,0:T(8,128)S(1)}, f32[32,8,16,64]{3,2,1,0:T(8,128)}, f32[32,8,65,64]{2,3,1,0:T(8,128)}, f32[32,8,16,64]{3,2,1,0:T(8...) while((s32[]{:T(128)}, f32[8,65,64]{1,2,0:T(8,128)S(1)}, ...), condition=%wide.region_6.7_spmd.clone.clone, body=%wide.region_5.6_spmd.clone.sunk.clone | while | flops 22418560 | bytes 1732721 | solution.py:82
  504.7 6.1 all-reduce.9
  510.8 5.0 multiply_convert_fusion.3
  518.4 34.2 %reduce-scatter.5.cloned.1.call-done = bf16[128,2048]{1,0:T(8,128)(2,1)} async-done(((bf16[512,2048]{1,0:T(8,128)(2,1)}), bf16[128,2048]{1,0:T(8,128)(2,1)}) %reduce-scatter.5.cloned.1.call-update) | async-done | bytes 524304 | tf_op jit(solution)/shard_map/reduce_scatter | solution.py:196
  556.6 22.1 all-gather.7.cloned.1.call-done
  578.8 8.1 fusion.139
  586.8 7.7 fusion.138
  594.5 8.4 all-gather.9.cloned.1.call-done
  602.9 10.3 multiply_convert_fusion
  613.1 6.4 fusion.140
  619.6 7.6 convolution_add_fusion.7
  627.3 44.6 %reduce-scatter.9.cloned.1.call-done = f32[128,2048]{1,0:T(8,128)} async-done(((f32[512,2048]{1,0:T(8,128)}), f32[128,2048]{1,0:T(8,128)}) %reduce-scatter.9.cloned.1.call-update) | async-done | bytes 1048592 | tf_op jit(solution)/shard_map/reduce_scatter | solution.py:226
  677.7 20.0 all-gather.11.cloned.1.call-done
  697.7 6.2 multiply_reduce_fusion.4
  703.9 6.0 all-reduce.8
  716.1 201.9 %while.98 = (s32[]{:T(128)}, f32[8,65,64]{1,2,0:T(8,128)S(1)}, f32[32,8,16,64]{3,2,1,0:T(8,128)}, f32[32,8,16]{2,1,0:T(8,128)}, f32[32,8,16,64]{3,2,1,0:T(8,128)}, /*index=5*/f32[32,8,16,64]{3,2,1,0:T(8,128)}) while((s32[]{:T(128)}, f32[8,65,64]{1,2,0:T(8,128)S(1)}, f32[32,8,16,64]{3,2,1,0:T(8,128)}, ...), condition=%wide.region_21.22_spmd.clone.clone, body=%wide.region_20.21_spmd.clone.sunk.clone | while | flops 48552844 | bytes 1615035 | solution.py:100
  918.0 69.7 %while.94 = (s32[]{:T(128)}, f32[8,65,64]{1,2,0:T(8,128)S(1)}, f32[8,65,65]{2,1,0:T(8,128)S(1)}, f32[8,65,64]{1,2,0:T(8,128)S(1)}) while((s32[]{:T(128)}, f32[8,65,64]{1,2,0:T(8,128)S(1)}, f32[8,65,65]{2,1,0:T(8,128)S(1)}, f32[8,65,64]{1,2,0:T(8,128)S(1)}) %tuple.220), condition=%wide.region_23.24_spmd.clone, body=%wide.region_22.23_spmd.sunk.clone | while | flops 25991680 | bytes 1067133 | solution.py:258
  920.0 8.4 collective-permute-done.1
  930.3 8.0 collective-permute-done.1
  940.2 7.6 collective-permute-done.1
  949.7 7.9 collective-permute-done.1
  959.4 7.9 collective-permute-done.1
  969.2 8.5 collective-permute-done.1
  979.6 8.1 collective-permute-done.1
  987.8 335.0 %while.95 = (s32[]{:T(128)}, f32[8,65,64]{1,2,0:T(8,128)S(1)}, bf16[32,8,16,64]{3,2,1,0:T(8,128)(2,1)S(1)}, bf16[32,8,16,64]{3,2,1,0:T(8,128)(2,1)}, bf16[32,8,1...) while((s32[]{:T(128)}, f32[8,65,64]{1,2,0:T(8,128)S(1)}, ...), condition=%wide.region_27.28_spmd.clone, body=%wide.region_24.27_spmd.sunk.clone | while | flops 52939520 | bytes 3343009 | solution.py:82
  1345.7 7.2 convolution_convert_fusion.9
  1353.0 8.2 convolution_convert_fusion.2
  1361.2 5.1 convolution_convert_fusion
  1366.4 4.8 convolution_convert_fusion.1
  1372.1 4.5 convolution_convert_fusion.3
  1389.6 36.2 %all-reduce.10 = (bf16[2048,8]{0,1:T(8,128)(2,1)S(1)}, bf16[8]{0:T(256)(128)(2,1)S(1)}, bf16[8]{0:T(256)(128)(2,1)S(1)}, bf16[512]{0:T(512)(128)(2,1)S(1)}, bf16[512]{0:T(512)(128)(2,1)S(1)}) all-reduce(bf16[2048,8]{0,1:T(8,128)(2,1)S(1)} %convolution_convert_fusion.10, ...), channel_id=1, replica_groups=mesh['seq'=8,'head'=4] {'seq'}, use_global_device_ids=true, to_apply=%region_36.37 | all-reduce | flops 17424 | bytes 69696 | tf_op jit(solution)/shard_map/psum | solution.py:299
  1430.1 42.8 %all-reduce.7 = (f32[2048]{0:T(1024)}, f32[2048]{0:T(1024)}) all-reduce(f32[2048]{0:T(1024)S(1)} %get-tuple-element.720, f32[2048]{0:T(1024)S(1)} %get-tuple-element.715), channel_id=1, replica_groups=mesh['seq'=8,'head'=4] {'seq','head'}, use_global_device_ids=true, to_apply=%region_31.32 | all-reduce | flops 4096 | bytes 32768 | tf_op jit(solution)/shard_map/psum | solution.py:310
  1476.0 770.8 %all-reduce.14.cloned.1.call-done = (bf16[2048,512]{1,0:T(8,128)(2,1)}, bf16[2048,512]{1,0:T(8,128)(2,1)}, bf16[2048,512]{1,0:T(8,128)(2,1)}, bf16[2048,512]{1,0...) async-done(((bf16[2048,512]{1,0:T(8,128)(2,1)}, ...) | async-done | bytes 27460624 | tf_op jit(solution)/shard_map/psum | solution.py:295
  2266.1 5.9 convert_element_type.237
  2272.0 5.9 convert_element_type.239
  2278.0 5.9 convert_element_type.241
  (1791 shorter events, 1050.3 us)
Async XLA Ops:
  7.2 508.6 %copy-start = (bf16[512,2048]{1,0:T(8,128)(2,1)S(1)}, bf16[512,2048]{1,0:T(8,128)(2,1)}, u32[]{:S(2)}) copy-start(bf16[512,2048]{1,0:T(8,128)(2,1)} %param.44) | copy-start | bytes 6291460
  7.2 29.0 %copy-start.30 = (bf16[2048,8]{0,1:T(8,128)(2,1)S(1)}, bf16[2048,8]{0,1:T(8,128)(2,1)}, u32[]{:S(2)}) copy-start(bf16[2048,8]{0,1:T(8,128)(2,1)} %param.37) | copy-start | bytes 98308
  7.2 29.0 %copy-start.38 = (f32[8]{0:T(128)S(1)}, f32[8]{0:T(128)}, u32[]{:S(2)}) copy-start(f32[8]{0:T(128)} %param.39) | copy-start | bytes 100
  7.2 28.9 %copy-start.42 = (f32[8]{0:T(128)S(1)}, f32[8]{0:T(128)}, u32[]{:S(2)}) copy-start(f32[8]{0:T(128)} %param.38) | copy-start | bytes 100
  7.3 28.9 %all-gather.5.cloned.1.call-start = ((), (), s32[]{:S(2)}) async-start(), calls=%async_computation.4 | async-start | bytes 2621440 | tf_op jit(solution)/shard_map/all_gather | solution.py:154
  10.7 541.9 %reduce-scatter.5.cloned.1.call-start = ((), (), s32[]{:S(2)}) async-start(), calls=%async_computation.5 | async-start | bytes 2621440 | tf_op jit(solution)/shard_map/reduce_scatter | solution.py:196
  232.7 9.6 collective-permute-start
  243.6 9.7 collective-permute-start
  254.7 8.8 collective-permute-start
  264.9 9.3 collective-permute-start
  275.6 9.4 collective-permute-start
  286.3 9.4 collective-permute-start
  297.0 9.4 collective-permute-start
  502.0 8.9 copy-start.36
  502.0 8.9 copy-start.45
  518.4 34.2 %copy-start.2 = (bf16[128,2048]{1,0:T(8,128)(2,1)S(1)}, bf16[128,2048]{1,0:T(8,128)(2,1)}, u32[]{:S(2)}) copy-start(bf16[128,2048]{1,0:T(8,128)(2,1)} %param.31) | copy-start | bytes 1572868
  518.4 35.5 %copy-start.31 = (f32[2048]{0:T(1024)S(1)}, f32[2048]{0:T(1024)}, u32[]{:S(2)}) copy-start(f32[2048]{0:T(1024)} %param.45) | copy-start | bytes 24580
  518.4 60.4 %all-gather.7.cloned.1.call-start = ((), (), s32[]{:S(2)}) async-start(), calls=%async_computation.6 | async-start | bytes 2621440 | tf_op jit(solution)/shard_map/all_gather | solution.py:206
  556.0 46.9 %all-gather.9.cloned.1.call-start = ((), (), s32[]{:S(2)}) async-start(), calls=%async_computation.8 | async-start | bytes 2621440 | tf_op jit(solution)/shard_map/all_gather | solution.py:155
  556.6 115.3 %reduce-scatter.9.cloned.1.call-start = ((), (), s32[]{:S(2)}) async-start(), calls=%async_computation.9 | async-start | bytes 5242880 | tf_op jit(solution)/shard_map/reduce_scatter | solution.py:226
  578.8 8.1 copy-start.43
  613.1 6.4 copy-start.46
  613.1 6.5 copy-start.26
  627.2 44.7 %copy-start.5 = (bf16[128,2048]{1,0:T(8,128)(2,1)S(1)}, bf16[128,2048]{1,0:T(8,128)(2,1)}, u32[]{:S(2)}) copy-start(bf16[128,2048]{1,0:T(8,128)(2,1)} %reduce-scatter.5.cloned.1.call-done) | copy-start | bytes 1572868
  627.2 70.5 %all-gather.11.cloned.1.call-start = ((), (), s32[]{:S(2)}) async-start(), calls=%async_computation.10 | async-start | bytes 2621440 | tf_op jit(solution)/shard_map/all_gather | solution.py:239
  674.9 753.7 %reduce-scatter.11.cloned.1.call-start = ((), (), s32[]{:S(2)}) async-start(), calls=%async_computation.11 | async-start | bytes 2621440 | tf_op jit(solution)/shard_map/reduce_scatter | solution.py:281
  697.7 12.3 copy-start.37
  918.0 69.7 %copy-start.4 = (bf16[32,8,16,64]{3,2,1,0:T(8,128)(2,1)S(1)}, bf16[32,8,16,64]{3,2,1,0:T(8,128)(2,1)}, u32[]{:S(2)}) copy-start(bf16[32,8,16,64]{3,2,1,0:T(8,128)(2,1)} %copy-done.3) | copy-start | bytes 1572868
  918.7 9.7 collective-permute-start.1
  929.0 9.3 collective-permute-start.1
  938.9 8.9 collective-permute-start.1
  948.4 9.2 collective-permute-start.1
  958.1 9.2 collective-permute-start.1
  967.9 9.8 collective-permute-start.1
  978.3 9.4 collective-permute-start.1
  1330.5 8.0 copy-start.14
  1344.4 128.5 %reduce-scatter.7.cloned.1.call-start = ((), (), s32[]{:S(2)}) async-start(), calls=%async_computation.7 | async-start | bytes 2621440 | tf_op jit(solution)/shard_map/reduce_scatter | solution.py:212
  1352.9 8.3 copy-start.27
  1352.9 893.9 %all-reduce.14.cloned.1.call-start = ((), (), s32[]{:S(2)}) async-start(), calls=%async_computation.12 | async-start | bytes 55054336 | tf_op jit(solution)/shard_map/psum | solution.py:295
  1353.0 8.3 copy-start.44
  1387.2 41.5 %copy-start.32 = (f32[2048]{0:T(1024)S(1)}, f32[2048]{0:T(1024)}, u32[]{:S(2)}) copy-start(f32[2048]{0:T(1024)} %param.32) | copy-start | bytes 24580
  1387.2 41.5 %copy-start.34 = (f32[128]{0:T(128)S(1)}, f32[128]{0:T(128)}, u32[]{:S(2)}) copy-start(f32[128]{0:T(128)} %copy-done.33) | copy-start | bytes 1540
  1387.2 85.7 %copy-start.6 = (bf16[128,2048]{1,0:T(8,128)(2,1)S(1)}, bf16[128,2048]{1,0:T(8,128)(2,1)}, u32[]{:S(2)}) copy-start(bf16[128,2048]{1,0:T(8,128)(2,1)} %reduce-scatter.5.cloned.1.call-done) | copy-start | bytes 1572868
  1387.2 85.7 %copy-start.8 = (f32[128,2048]{1,0:T(8,128)S(1)}, f32[128,2048]{1,0:T(8,128)}, u32[]{:S(2)}) copy-start(f32[128,2048]{1,0:T(8,128)} %reduce-scatter.9.cloned.1.call-done) | copy-start | bytes 3145732
  1387.2 85.7 %copy-start.12 = (bf16[128,2048]{1,0:T(8,128)(2,1)S(1)}, bf16[128,2048]{1,0:T(8,128)(2,1)}, u32[]{:S(2)}) copy-start(bf16[128,2048]{1,0:T(8,128)(2,1)} %param.49) | copy-start | bytes 1572868
  2257.0 9.1 slice-start.4
  2263.4 8.6 slice-start.2
  2266.1 11.8 slice-start
  (31 other events, 105.6 us)
Sparse Core Ops, SparseCore 0:
  10.9 25.2 all-gather.4
  518.5 34.0 reduce-scatter.4
  556.1 22.5 all-gather.6
  580.2 22.5 all-gather.8
  627.3 44.4 reduce-scatter.8
  675.0 22.5 all-gather.10
  1344.5 33.6 reduce-scatter.10
  1381.4 31.4 reduce-scatter.6
  1421.0 825.7 all-reduce.13
where the time goes:
time: 2320 us; the launch traced here: 2290 us
  waiting for transfers between devices  1010 us (44%)
  matrix products  658 us (28%)
  local copies, waits for them, and re-layouts  380 us (16%)
  blocking collectives  91.2 us (4%)
  other arithmetic  81.4 us (4%)
  starting transfers between devices  42.1 us (2%)
    psum x1, waiting for transfers between devices, body(): lax.psum(query_grad.astype(jnp.bfloat16), 'seq').astype(jnp.float32)  771 us
    squeeze x256, local copies, waits for them, and re-layouts, segment_map(): lax.scan(turn, (identity, zero_state), (key_blocks, value_blocks, rate_bl...  213 us
    dot_general x128, matrix products, inner_block(): jnp.einsum('hmi,hio->hmo', key_aug, inner_state, precision=HIGHEST)  90.1 us
    ppermute x14, waiting for transfers between devices, passed_along(): return lax.ppermute(shard, axis, pairs)  89.2 us
    dot_general x64, matrix products, step_matrix_of(): jnp.einsum('hni,hnj->hij', weighted_keys, key_aug, precision=HIGHEST)  53.1 us
    dot_general x96, matrix products, inner_block(): jnp.einsum('hni,hno->hio', key_aug * rate_block[:, :, None], errors, prec...  52.9 us
    dot_general x32, matrix products, turn(): jnp.einsum('hni,hno->hio', weighted_keys, value_block - key_block, precis...  47.8 us
  transfers between devices with their start and end apart: 23, of which 21 were waited for; matrix products, arithmetic and copies ran while one was open for 3% of the time, Pallas kernels for 0%

commit v1 on v0

--- a/solution.py
+++ b/solution.py
@@ -292,7 +292,7 @@
         scaled_in - unit_in * jnp.mean(scaled_in * unit_in, axis=-1, keepdims=True)
     )
     summed = (
-        lax.psum(query_grad.astype(jnp.bfloat16), "seq").astype(jnp.float32),
+        jnp.sum(lax.all_gather(query_grad.astype(jnp.bfloat16), "seq"), axis=0).astype(jnp.float32),
         lax.psum(key_grad.astype(jnp.bfloat16), "seq").astype(jnp.float32),
         lax.psum(value_grad.astype(jnp.bfloat16), "seq").astype(jnp.float32),
         lax.psum(gate_grad.astype(jnp.bfloat16), "seq").astype(jnp.float32),

time: 2320 us -> 2470 us (1.065)
  waiting for transfers between devices: 1010 us -> 1150 us
    all_gather x0 -> x1, waiting for transfers between devices: none -> 194 us  [body(): lax.all_gather(query_grad.astype(jnp.bfloat16), 'seq')]
    psum x1, waiting for transfers between devices: 771 us -> 709 us  [body(): lax.psum(key_grad.astype(jnp.bfloat16), 'seq').astype(jnp.float32)]
  transfers between devices with their start and end apart: 23 -> 24, of which waited for: 21 -> 22; matrix products, arithmetic and copies ran while one was open for 3% -> 4% of each run, Pallas kernels for 0% -> 0%
where the time goes in v1:
time: 2470 us; the launch traced here: 2440 us
  waiting for transfers between devices  1150 us (47%)
  matrix products  658 us (27%)
  local copies, waits for them, and re-layouts  379 us (15%)
  other arithmetic  93.9 us (4%)
  blocking collectives  91.9 us (4%)
  starting transfers between devices  42 us (2%)
    psum x1, waiting for transfers between devices, body(): lax.psum(key_grad.astype(jnp.bfloat16), 'seq').astype(jnp.float32)  709 us
    squeeze x256, local copies, waits for them, and re-layouts, segment_map(): lax.scan(turn, (identity, zero_state), (key_blocks, value_blocks, rate_bl...  213 us
    all_gather x1, waiting for transfers between devices, body(): lax.all_gather(query_grad.astype(jnp.bfloat16), 'seq')  194 us
    dot_general x128, matrix products, inner_block(): jnp.einsum('hmi,hio->hmo', key_aug, inner_state, precision=HIGHEST)  90.1 us
    ppermute x14, waiting for transfers between devices, passed_along(): return lax.ppermute(shard, axis, pairs)  89.3 us
    dot_general x64, matrix products, step_matrix_of(): jnp.einsum('hni,hnj->hij', weighted_keys, key_aug, precision=HIGHEST)  53.1 us
    dot_general x96, matrix products, inner_block(): jnp.einsum('hni,hno->hio', key_aug * rate_block[:, :, None], errors, prec...  52.8 us
  transfers between devices with their start and end apart: 24, of which 22 were waited for; matrix products, arithmetic and copies ran while one was open for 4% of the time, Pallas kernels for 0%

profile of v1, /device:TPU:0, one launch (start us, length us, event | category | flops | bytes accessed | tf_op | source)
XLA Modules:
  0.0 2435.2 jit_solution(8103800803931328120)
XLA Ops:
  11.3 24.9 %all-gather.7.cloned.1.call-done = bf16[512,2048]{1,0:T(8,128)(2,1)} async-done(((bf16[128,2048]{1,0:T(8,128)(2,1)}), bf16[512,2048]{1,0:T(8,128)(2,1)}) %all-gather.7.cloned.1.call-update) | async-done | bytes 2097168 | tf_op jit(solution)/shard_map/all_gather | solution.py:154
  62.0 5.2 copy_bitcast_fusion.2
  67.1 164.1 %while.97 = (s32[]{:T(128)}, f32[8,65,65]{2,1,0:T(8,128)S(1)}, f32[8,65,64]{1,2,0:T(8,128)S(1)}, f32[32,8,16,64]{3,2,1,0:T(8,128)}, f32[32,8,16]{2,1,0:T(8,128)}, /*index=5*/f32[32,8,16,64]{3,2,1,0:T(8,128)}) while((s32[]{:T(128)}, f32[8,65,65]{2,1,0:T(8,128)S(1)}, f32[8,65,64]{1,2,0:T(8,128)S(1)}, ...), condition=%wide.region_2.3_spmd.clone.clone, body=%wide.region_1.2_spmd.clone.sunk.clone | while | flops 65335404 | bytes 1942347 | solution.py:52
  231.3 75.0 %while.93 = (s32[]{:T(128)}, f32[8,65,64]{1,2,0:T(8,128)S(1)}, pred[]{:T(512)}, f32[8,65,65]{2,1,0:T(8,128)S(1)}, f32[8,65,64]{1,2,0:T(8,128)S(1)}, /*index=5*/f32[8,65,64]{1,2,0:T(8,128)S(1)}) while((s32[]{:T(128)}, f32[8,65,64]{1,2,0:T(8,128)S(1)}, pred[]{:T(512)}, f32[8,65,65]{2,1,0:T(8,128)S(1)}, f32[8,65,64]{1,2,0:T(8,128)S(1)}, ...), condition=%wide.region_4.5_spmd.clone, body=%wide.region_3.4_spmd.sunk.clone | while | flops 26024960 | bytes 1466510 | solution.py:182
  235.9 6.3 collective-permute-done
  247.8 5.5 collective-permute-done
  264.8 5.1 collective-permute-start
  275.5 5.2 collective-permute-start
  286.2 5.2 collective-permute-start
  296.9 5.2 collective-permute-start
  306.3 189.6 %while.96 = (s32[]{:T(128)}, f32[8,65,64]{1,2,0:T(8,128)S(1)}, f32[32,8,16,64]{3,2,1,0:T(8,128)}, f32[32,8,65,64]{2,3,1,0:T(8,128)}, f32[32,8,16,64]{3,2,1,0:T(8...) while((s32[]{:T(128)}, f32[8,65,64]{1,2,0:T(8,128)S(1)}, ...), condition=%wide.region_6.7_spmd.clone.clone, body=%wide.region_5.6_spmd.clone.sunk.clone | while | flops 22418560 | bytes 1732721 | solution.py:82
  504.6 6.2 all-reduce.9
  510.8 5.0 multiply_convert_fusion.3
  519.3 34.2 %reduce-scatter.5.cloned.1.call-done = bf16[128,2048]{1,0:T(8,128)(2,1)} async-done(((bf16[512,2048]{1,0:T(8,128)(2,1)}), bf16[128,2048]{1,0:T(8,128)(2,1)}) %reduce-scatter.5.cloned.1.call-update) | async-done | bytes 524304 | tf_op jit(solution)/shard_map/reduce_scatter | solution.py:196
  557.4 22.1 all-gather.9.cloned.1.call-done
  579.5 8.1 fusion.139
  587.6 7.7 fusion.138
  595.3 8.4 all-gather.11.cloned.1.call-done
  603.7 10.3 multiply_convert_fusion
  613.9 6.4 fusion.140
  620.4 7.6 convolution_add_fusion.7
  628.0 44.6 %reduce-scatter.9.cloned.1.call-done = f32[128,2048]{1,0:T(8,128)} async-done(((f32[512,2048]{1,0:T(8,128)}), f32[128,2048]{1,0:T(8,128)}) %reduce-scatter.9.cloned.1.call-update) | async-done | bytes 1048592 | tf_op jit(solution)/shard_map/reduce_scatter | solution.py:226
  678.5 20.0 all-gather.13.cloned.1.call-done
  698.5 6.2 multiply_reduce_fusion.4
  704.7 6.0 all-reduce.8
  716.8 201.9 %while.98 = (s32[]{:T(128)}, f32[8,65,64]{1,2,0:T(8,128)S(1)}, f32[32,8,16,64]{3,2,1,0:T(8,128)}, f32[32,8,16]{2,1,0:T(8,128)}, f32[32,8,16,64]{3,2,1,0:T(8,128)}, /*index=5*/f32[32,8,16,64]{3,2,1,0:T(8,128)}) while((s32[]{:T(128)}, f32[8,65,64]{1,2,0:T(8,128)S(1)}, f32[32,8,16,64]{3,2,1,0:T(8,128)}, ...), condition=%wide.region_21.22_spmd.clone.clone, body=%wide.region_20.21_spmd.clone.sunk.clone | while | flops 48552844 | bytes 1615035 | solution.py:100
  918.8 69.7 %while.94 = (s32[]{:T(128)}, f32[8,65,64]{1,2,0:T(8,128)S(1)}, f32[8,65,65]{2,1,0:T(8,128)S(1)}, f32[8,65,64]{1,2,0:T(8,128)S(1)}) while((s32[]{:T(128)}, f32[8,65,64]{1,2,0:T(8,128)S(1)}, f32[8,65,65]{2,1,0:T(8,128)S(1)}, f32[8,65,64]{1,2,0:T(8,128)S(1)}) %tuple.220), condition=%wide.region_23.24_spmd.clone, body=%wide.region_22.23_spmd.sunk.clone | while | flops 25991680 | bytes 1067133 | solution.py:258
  920.7 8.4 collective-permute-done.1
  931.0 8.0 collective-permute-done.1
  940.9 7.6 collective-permute-done.1
  950.4 7.9 collective-permute-done.1
  960.2 7.9 collective-permute-done.1
  970.0 8.5 collective-permute-done.1
  980.4 8.1 collective-permute-done.1
  988.5 334.8 %while.95 = (s32[]{:T(128)}, f32[8,65,64]{1,2,0:T(8,128)S(1)}, bf16[32,8,16,64]{3,2,1,0:T(8,128)(2,1)S(1)}, bf16[32,8,16,64]{3,2,1,0:T(8,128)(2,1)}, bf16[32,8,1...) while((s32[]{:T(128)}, f32[8,65,64]{1,2,0:T(8,128)S(1)}, ...), condition=%wide.region_27.28_spmd.clone, body=%wide.region_24.27_spmd.sunk.clone | while | flops 52939520 | bytes 3343009 | solution.py:82
  1343.5 7.2 convolution_convert_fusion.9
  1350.8 8.2 convolution_convert_fusion.2
  1359.1 5.1 convolution_convert_fusion
  1364.2 4.8 convolution_convert_fusion.1
  1369.9 4.6 convolution_convert_fusion.3
  1387.6 36.1 %all-reduce.10 = (bf16[2048,8]{0,1:T(8,128)(2,1)S(1)}, bf16[8]{0:T(256)(128)(2,1)S(1)}, bf16[8]{0:T(256)(128)(2,1)S(1)}, bf16[512]{0:T(512)(128)(2,1)S(1)}, bf16[512]{0:T(512)(128)(2,1)S(1)}) all-reduce(bf16[2048,8]{0,1:T(8,128)(2,1)S(1)} %convolution_convert_fusion.10, ...), channel_id=1, replica_groups=mesh['seq'=8,'head'=4] {'seq'}, use_global_device_ids=true, to_apply=%region_36.37 | all-reduce | flops 17424 | bytes 69696 | tf_op jit(solution)/shard_map/psum | solution.py:299
  1428.0 43.6 %all-reduce.7 = (f32[2048]{0:T(1024)}, f32[2048]{0:T(1024)}) all-reduce(f32[2048]{0:T(1024)S(1)} %get-tuple-element.720, f32[2048]{0:T(1024)S(1)} %get-tuple-element.715), channel_id=1, replica_groups=mesh['seq'=8,'head'=4] {'seq','head'}, use_global_device_ids=true, to_apply=%region_31.32 | all-reduce | flops 4096 | bytes 32768 | tf_op jit(solution)/shard_map/psum | solution.py:310
  1474.7 709.3 %all-reduce.14.cloned.1.call-done = (bf16[2048,512]{1,0:T(8,128)(2,1)}, bf16[2048,512]{1,0:T(8,128)(2,1)}, bf16[2048,512]{1,0:T(8,128)(2,1)}, bf16[8,65,64]{2,0,...) async-done(((bf16[2048,512]{1,0:T(8,128)(2,1)}, bf16[2048,512]{1,0:T(8,128)(2,1)}, ...) | async-done | bytes 25363472 | tf_op jit(solution)/shard_map/psum | solution.py:296
  2200.9 5.9 convert_element_type.239
  2206.9 5.9 convert_element_type.241
  2212.8 5.9 convert_element_type.243
  2219.3 194.1 %all-gather.15.cloned.1.call-done = bf16[16384,512]{1,0:T(8,128)(2,1)} async-done(((bf16[2048,512]{1,0:T(8,128)(2,1)}), bf16[16384,512]{1,0:T(8,128)(2,1)}) %all-gather.15.cloned.1.call-update) | async-done | bytes 16777232 | tf_op jit(solution)/shard_map/all_gather | solution.py:295
  2413.4 10.7 reduce_sum.194
  (1795 shorter events, 1059.5 us)
Async XLA Ops:
  7.2 509.4 %copy-start = (bf16[512,2048]{1,0:T(8,128)(2,1)S(1)}, bf16[512,2048]{1,0:T(8,128)(2,1)}, u32[]{:S(2)}) copy-start(bf16[512,2048]{1,0:T(8,128)(2,1)} %param.44) | copy-start | bytes 6291460
  7.2 29.0 %copy-start.30 = (bf16[2048,8]{0,1:T(8,128)(2,1)S(1)}, bf16[2048,8]{0,1:T(8,128)(2,1)}, u32[]{:S(2)}) copy-start(bf16[2048,8]{0,1:T(8,128)(2,1)} %param.37) | copy-start | bytes 98308
  7.2 29.0 %copy-start.38 = (f32[8]{0:T(128)S(1)}, f32[8]{0:T(128)}, u32[]{:S(2)}) copy-start(f32[8]{0:T(128)} %param.39) | copy-start | bytes 100
  7.2 28.9 %copy-start.42 = (f32[8]{0:T(128)S(1)}, f32[8]{0:T(128)}, u32[]{:S(2)}) copy-start(f32[8]{0:T(128)} %param.38) | copy-start | bytes 100
  7.3 28.9 %all-gather.7.cloned.1.call-start = ((), (), s32[]{:S(2)}) async-start(), calls=%async_computation.4 | async-start | bytes 2621440 | tf_op jit(solution)/shard_map/all_gather | solution.py:154
  8.7 29.8 %copy-start.33 = (f32[128]{0:T(128)}, f32[128]{0:T(128)S(1)}, u32[]{:S(2)}) copy-start(f32[128]{0:T(128)S(1)} %add_rsqrt_fusion.2) | copy-start | bytes 1540
  10.7 542.7 %reduce-scatter.5.cloned.1.call-start = ((), (), s32[]{:S(2)}) async-start(), calls=%async_computation.5 | async-start | bytes 2621440 | tf_op jit(solution)/shard_map/reduce_scatter | solution.py:196
  232.6 9.6 collective-permute-start
  243.6 9.7 collective-permute-start
  254.7 8.8 collective-permute-start
  264.8 9.3 collective-permute-start
  275.5 9.4 collective-permute-start
  286.2 9.4 collective-permute-start
  296.9 9.4 collective-permute-start
  501.9 8.9 copy-start.36
  501.9 8.9 copy-start.45
  519.2 34.2 %copy-start.2 = (bf16[128,2048]{1,0:T(8,128)(2,1)S(1)}, bf16[128,2048]{1,0:T(8,128)(2,1)}, u32[]{:S(2)}) copy-start(bf16[128,2048]{1,0:T(8,128)(2,1)} %param.31) | copy-start | bytes 1572868
  519.2 35.5 %copy-start.31 = (f32[2048]{0:T(1024)S(1)}, f32[2048]{0:T(1024)}, u32[]{:S(2)}) copy-start(f32[2048]{0:T(1024)} %param.45) | copy-start | bytes 24580
  519.2 60.3 %all-gather.9.cloned.1.call-start = ((), (), s32[]{:S(2)}) async-start(), calls=%async_computation.6 | async-start | bytes 2621440 | tf_op jit(solution)/shard_map/all_gather | solution.py:206
  556.8 46.9 %all-gather.11.cloned.1.call-start = ((), (), s32[]{:S(2)}) async-start(), calls=%async_computation.8 | async-start | bytes 2621440 | tf_op jit(solution)/shard_map/all_gather | solution.py:155
  557.4 115.3 %reduce-scatter.9.cloned.1.call-start = ((), (), s32[]{:S(2)}) async-start(), calls=%async_computation.9 | async-start | bytes 5242880 | tf_op jit(solution)/shard_map/reduce_scatter | solution.py:226
  579.5 8.1 copy-start.43
  628.0 44.7 %copy-start.5 = (bf16[128,2048]{1,0:T(8,128)(2,1)S(1)}, bf16[128,2048]{1,0:T(8,128)(2,1)}, u32[]{:S(2)}) copy-start(bf16[128,2048]{1,0:T(8,128)(2,1)} %reduce-scatter.5.cloned.1.call-done) | copy-start | bytes 1572868
  628.0 70.5 %all-gather.13.cloned.1.call-start = ((), (), s32[]{:S(2)}) async-start(), calls=%async_computation.10 | async-start | bytes 2621440 | tf_op jit(solution)/shard_map/all_gather | solution.py:239
  675.7 750.8 %reduce-scatter.11.cloned.1.call-start = ((), (), s32[]{:S(2)}) async-start(), calls=%async_computation.11 | async-start | bytes 2621440 | tf_op jit(solution)/shard_map/reduce_scatter | solution.py:281
  698.5 12.3 copy-start.37
  918.8 69.7 %copy-start.4 = (bf16[32,8,16,64]{3,2,1,0:T(8,128)(2,1)S(1)}, bf16[32,8,16,64]{3,2,1,0:T(8,128)(2,1)}, u32[]{:S(2)}) copy-start(bf16[32,8,16,64]{3,2,1,0:T(8,128)(2,1)} %copy-done.3) | copy-start | bytes 1572868
  919.4 9.7 collective-permute-start.1
  929.7 9.3 collective-permute-start.1
  939.6 8.9 collective-permute-start.1
  949.1 9.2 collective-permute-start.1
  958.9 9.2 collective-permute-start.1
  968.7 9.8 collective-permute-start.1
  979.1 9.4 collective-permute-start.1
  1342.2 129.4 %reduce-scatter.7.cloned.1.call-start = ((), (), s32[]{:S(2)}) async-start(), calls=%async_computation.7 | async-start | bytes 2621440 | tf_op jit(solution)/shard_map/reduce_scatter | solution.py:212
  1350.7 8.3 copy-start.27
  1350.7 833.3 %all-reduce.14.cloned.1.call-start = ((), (), s32[]{:S(2)}) async-start(), calls=%async_computation.13 | async-start | bytes 50860032 | tf_op jit(solution)/shard_map/psum | solution.py:296
  1350.8 8.3 copy-start.44
  1382.4 1031.0 %all-gather.15.cloned.1.call-start = ((), (), s32[]{:S(2)}) async-start(), calls=%async_computation.12 | async-start | bytes 18874368 | tf_op jit(solution)/shard_map/all_gather | solution.py:295
  1385.1 41.4 %copy-start.32 = (f32[2048]{0:T(1024)S(1)}, f32[2048]{0:T(1024)}, u32[]{:S(2)}) copy-start(f32[2048]{0:T(1024)} %param.32) | copy-start | bytes 24580
  1385.1 41.4 %copy-start.34 = (f32[128]{0:T(128)S(1)}, f32[128]{0:T(128)}, u32[]{:S(2)}) copy-start(f32[128]{0:T(128)} %copy-done.33) | copy-start | bytes 1540
  1385.1 86.4 %copy-start.6 = (bf16[128,2048]{1,0:T(8,128)(2,1)S(1)}, bf16[128,2048]{1,0:T(8,128)(2,1)}, u32[]{:S(2)}) copy-start(bf16[128,2048]{1,0:T(8,128)(2,1)} %reduce-scatter.5.cloned.1.call-done) | copy-start | bytes 1572868
  1385.1 86.4 %copy-start.8 = (f32[128,2048]{1,0:T(8,128)S(1)}, f32[128,2048]{1,0:T(8,128)}, u32[]{:S(2)}) copy-start(f32[128,2048]{1,0:T(8,128)} %reduce-scatter.9.cloned.1.call-done) | copy-start | bytes 3145732
  1385.1 86.4 %copy-start.12 = (bf16[128,2048]{1,0:T(8,128)(2,1)S(1)}, bf16[128,2048]{1,0:T(8,128)(2,1)}, u32[]{:S(2)}) copy-start(bf16[128,2048]{1,0:T(8,128)(2,1)} %param.49) | copy-start | bytes 1572868
  2191.0 9.9 slice-start.4
  2198.3 8.6 slice-start.2
  2200.9 11.8 slice-start
  2413.4 14.9 copy-start.1
  (32 other events, 112.0 us)
Sparse Core Ops, SparseCore 0:
  10.9 25.2 all-gather.6
  519.3 34.0 reduce-scatter.4
  556.9 22.5 all-gather.8
  581.0 22.5 all-gather.10
  628.1 44.4 reduce-scatter.8
  675.8 22.5 all-gather.12
  1342.3 33.5 reduce-scatter.10
  1379.2 31.4 reduce-scatter.6
  1418.1 765.9 all-reduce.13
  2186.8 226.4 all-gather.14
